TPU v7x, 32 devices: a whole 2x2x4 slice. The times are simulated.
32 devices in a mesh: row: 4 (over y, x), col: 2 (over core), dp: 4 (over z).
Axes of the slice: x: 2, y: 2, z: 4, core: 2. Of those that a mesh axis runs over, the one named last changes fastest.
Arguments:
- out_grad: bfloat16 [4, 128, 4096], P('dp', 'col', 'row'), may hold values from -6 to 6
- saved_hidden: bfloat16 [4, 128, 14336], P('dp', 'row', 'col'), may hold values from -6 to 6
- down_weight: bfloat16 [14336, 4096], P(('col', 'dp'), 'row'), may hold values from -0.046875 to 0.046875
Outputs:
- hidden_grad: bfloat16 [4, 128, 14336], P('dp', 'row', 'col')
- weight_grad: bfloat16 [14336, 4096], P(('col', 'dp'), 'row')
All inputs are finite; a program needn't handle non-finite values.
Results may differ from a plain program's by a relative error of at most 0.009.
Values may be sent and summed in bfloat16 or wider, within the bound.
A program may use at most 64 MiB of HBM per device.

v0:
```python
import jax
import jax.numpy as jnp
from jax import lax
from jax.sharding import PartitionSpec as P


def on_device(out_grad, saved_hidden, down_weight):
    grad_local = out_grad[0]
    hidden_local = saved_hidden[0]
    units = down_weight.shape[0]
    width = down_weight.shape[1]
    grad_replica = lax.all_gather(grad_local, "col", axis=0, tiled=True)
    grad_all = lax.all_gather(grad_replica[:, None, :], "dp", axis=1, tiled=True)
    tok_count = grad_all.shape[0]
    replica_count = grad_all.shape[1]
    local_tokens = hidden_local.shape[0]
    hidden_units = lax.all_to_all(
        hidden_local[:, None, :], "dp", split_axis=2, concat_axis=1, tiled=True
    )
    factor = jnp.float32(1.0) / jnp.sqrt(jnp.float32(tok_count * replica_count))
    flat_grad = grad_all.reshape(tok_count * replica_count, width)
    rows = flat_grad
    summed = lax.psum_scatter(
        lax.dot_general(
            rows, down_weight, (((1,), (1,)), ((), ())), preferred_element_type=jnp.float32
        ).astype(jnp.bfloat16),
        "row",
        scatter_dimension=0,
        tiled=True,
    )
    local_grad = summed.reshape(local_tokens, replica_count, units)
    returned = lax.all_to_all(local_grad, "dp", split_axis=1, concat_axis=2, tiled=True)
    hidden_grad = returned.reshape(1, local_tokens, -1)
    rows = grad_all
    left = lax.all_gather(hidden_units, "row", axis=0, tiled=True).reshape(-1, units)
    right = rows.reshape(-1, width)
    total = lax.dot_general(
        left, right, (((0,), (0,)), ((), ())), preferred_element_type=jnp.float32
    )
    weight_grad = (total * factor).astype(jnp.bfloat16)
    return (hidden_grad, weight_grad)


def solution(mesh):
    in_specs = (P("dp", "col", "row"), P("dp", "row", "col"), P(("col", "dp"), "row"))
    out_specs = (P("dp", "row", "col"), P(("col", "dp"), "row"))
    return jax.shard_map(
        on_device, mesh=mesh, in_specs=in_specs, out_specs=out_specs, check_vma=False
    )
```

profile of v0, /device:TPU:0, one launch (start us, length us, event | category | flops | bytes accessed | tf_op | source)
XLA Modules:
  0.0 169.9 jit_solution(11268376020256023476)
XLA Ops:
  7.2 0.0 all-gather.7.cloned.1.call-start
  7.2 2.3 %all-gather = bf16[1,128,1024]{2,1,0:T(8,128)(2,1)S(1)} all-gather(bf16[1,64,1024]{2,1,0:T(8,128)(2,1)} %param.3), channel_id=2, replica_groups=mesh['row'=4,'col'=2,'dp'=4] {'col'}, dimensions={1}, use_global_device_ids=true | all-gather | bytes 393216 | tf_op jit(solution)/shard_map/all_gather | solution.py:12
  9.5 0.8 copy.19
  10.4 0.0 all-gather.7.cloned.1.call-update
  10.4 0.0 reduce-scatter.2.cloned.1.call-start
  10.5 30.7 %all-gather.7.cloned.1.call-done = bf16[1,128,4096]{1,2,0:T(8,128)(2,1)} async-done(((bf16[1,128,1024]{1,2,0:T(8,128)(2,1)}), bf16[1,128,4096]{1,2,0:T(8,128)(2,1)}) %all-gather.7.cloned.1.call-update) | async-done | bytes 1048592 | tf_op jit(solution)/shard_map/all_gather | solution.py:13
  41.1 1.5 copy.20
  42.6 0.7 reshape.22
  43.3 0.0 copy-start.1
  43.3 5.4 %convolution_convert_fusion = bf16[512,1792]{1,0:T(8,128)(2,1)} fusion(bf16[512,1024]{1,0:T(8,128)(2,1)S(1)} %reshape.22, bf16[1792,1024]{1,0:T(8,128)(2,1)} %param.5), kind=kOutput, calls=%fused_computation.2 | convolution fusion | flops 1879965696 | bytes 6553600 | tf_op jit(solution)/shard_map/dot_general | solution.py:24
  48.8 0.0 reduce-scatter.2.cloned.1.call-update
  48.8 0.0 all-gather.5.cloned.1.call-start
  48.8 0.0 copy-done.1
  48.8 5.9 %copy.23 = bf16[32,1,7168]{0,1,2:T(2,128)(2,1)} copy(bf16[32,1,7168]{2,0,1:T(8,128)(2,1)S(1)} %bitcast.17) | data formatting | bytes 917504 | tf_op jit(solution)/shard_map/broadcast_in_dim;squeeze | solution.py:18
  54.8 0.5 broadcast
  55.3 39.8 %reduce = bf16[7168,32]{1,0:T(8,128)(2,1)S(1)} reduce(bf16[7168,1,32]{2,1,0:T(2,128)(2,1)} %bitcast.14, bf16[]{:T(256)} %broadcast), dimensions={1}, to_apply=%bitcast.8.reduce_sub_computation | reduce | bytes 917506
  95.1 1.8 %reshape.29 = bf16[4,2,28672]{2,1,0:T(2,128)(2,1)S(1)} reshape(bf16[7168,32]{1,0:T(8,128)(2,1)S(1)} %reduce) | data formatting | bytes 917504
  96.8 15.8 %all_to_all.21 = bf16[4,2,28672]{2,1,0:T(2,128)(2,1)S(1)} all-to-all(bf16[4,2,28672]{2,1,0:T(2,128)(2,1)S(1)} %reshape.29), channel_id=1, replica_groups=mesh['row'=4,'col'=2,'dp'=4] {'dp'}, dimensions={0} | all-to-all | bytes 917504 | tf_op jit(solution)/shard_map/all_to_all | solution.py:17
  112.7 3.0 %reshape.30 = bf16[7168,1,32]{2,1,0:T(2,128)(2,1)} reshape(bf16[4,2,28672]{2,1,0:T(2,128)(2,1)S(1)} %all_to_all.21) | data formatting | bytes 917504
  115.7 7.1 %copy.24 = bf16[32,1,7168]{2,0,1:T(8,128)(2,1)S(1)} copy(bf16[32,1,7168]{0,1,2:T(2,128)(2,1)} %bitcast.15) | data formatting | bytes 917504 | tf_op jit(solution)/shard_map/all_to_all | solution.py:17
  122.8 0.3 all_to_all.8
  123.1 0.8 copy.25
  123.9 0.0 all-gather.5.cloned.1.call-update
  123.9 0.0 reduce-scatter.2.cloned.1.call-done
  124.0 1.1 reshape.23
  125.1 0.8 copy.21
  125.9 3.6 %all-to-all-start = ((bf16[32,4,1792]{2,0,1:T(8,128)(2,1)}), bf16[32,4,1792]{2,0,1:T(8,128)(2,1)S(1)}, u32[]{:S(2)}, u32[]{:S(2)}) async-start(bf16[32,4,1792]{2,0,1:T(8,128)(2,1)} %copy.21), calls=%async_computation.1 | async-start | bytes 917504 | tf_op jit(solution)/shard_map/all_to_all | solution.py:32
  129.6 26.9 %all-gather.5.cloned.1.call-done = bf16[128,4,1792]{2,0,1:T(8,128)(2,1)} async-done(((bf16[32,4,1792]{2,0,1:T(8,128)(2,1)}), bf16[128,4,1792]{2,0,1:T(8,128)(2,1)}) %all-gather.5.cloned.1.call-update) | async-done | bytes 1835024 | tf_op jit(solution)/shard_map/all_gather | solution.py:35
  156.5 5.5 %fusion = bf16[1792,1024]{1,0:T(8,128)(2,1)} fusion(bf16[128,4,1792]{2,0,1:T(8,128)(2,1)} %all-gather.5.cloned.1.call-done, bf16[128,4,1024]{0,2,1:T(8,128)(2,1)S(1)} %bitcast.16), kind=kOutput, calls=%fused_computation.1 | convolution fusion | flops 1882718208 | bytes 6553600 | tf_op jit(solution)/shard_map/dot_general | solution.py:37
  161.9 0.0 all-to-all-done
  161.9 0.4 copy.22
  162.3 1.1 reshape.24
  (2 shorter events, 0.0 us)
Async XLA Ops:
  7.2 34.0 %all-gather.7.cloned.1.call-start = ((), (), s32[]{:S(2)}) async-start(), calls=%async_computation.5 | async-start | bytes 1310720 | tf_op jit(solution)/shard_map/all_gather | solution.py:13
  10.4 113.5 %reduce-scatter.2.cloned.1.call-start = ((), (), s32[]{:S(2)}) async-start(), calls=%async_computation.3 | async-start | bytes 2293760 | tf_op jit(solution)/shard_map/reduce_scatter | solution.py:23
  43.3 5.5 %copy-start.1 = (bf16[1,32,7168]{2,1,0:T(8,128)(2,1)S(1)}, bf16[1,32,7168]{2,1,0:T(8,128)(2,1)}, u32[]{:S(2)}) copy-start(bf16[1,32,7168]{2,1,0:T(8,128)(2,1)} %param.4) | copy-start | bytes 1376260
  48.8 107.7 %all-gather.5.cloned.1.call-start = ((), (), s32[]{:S(2)}) async-start(), calls=%async_computation.4 | async-start | bytes 2293760 | tf_op jit(solution)/shard_map/all_gather | solution.py:35
  115.7 40.8 %copy-start = (bf16[1,128,4096]{1,2,0:T(8,128)(2,1)S(1)}, bf16[1,128,4096]{1,2,0:T(8,128)(2,1)}, u32[]{:S(2)}) copy-start(bf16[1,128,4096]{1,2,0:T(8,128)(2,1)} %all-gather.7.cloned.1.call-done) | copy-start | bytes 3145732
  125.9 36.0 %all-to-all-start = ((bf16[32,4,1792]{2,0,1:T(8,128)(2,1)}), bf16[32,4,1792]{2,0,1:T(8,128)(2,1)S(1)}, u32[]{:S(2)}, u32[]{:S(2)}) async-start(bf16[32,4,1792]{2,0,1:T(8,128)(2,1)} %copy.21), calls=%async_computation.1 | async-start | bytes 917504 | tf_op jit(solution)/shard_map/all_to_all | solution.py:32
Sparse Core Ops, SparseCore 0:
  10.5 30.5 all-gather.6
  48.9 32.4 reduce-scatter.1
  124.1 32.3 all-gather.4
where the time goes:
time: 170 us
  waiting for transfers between devices  57.7 us (34%)
  other arithmetic  39.8 us (23%)
  local copies, waits for them, and re-layouts  25.9 us (15%)
  blocking collectives  18.2 us (11%)
  between operations  13.8 us (8%)
  matrix products  10.9 us (6%)
  starting transfers between devices  3.77 us (2%)
    unnamed x1, other arithmetic  39.8 us
    all_gather x1, waiting for transfers between devices, on_device(): lax.all_gather(grad_replica[:, None, :], 'dp', axis=1, tiled=True)  30.7 us
    all_gather x1, waiting for transfers between devices, on_device(): lax.all_gather(hidden_units, 'row', axis=0, tiled=True).reshape(-1, units)  26.9 us
    all_to_all x1, blocking collectives, on_device(): lax.all_to_all(hidden_local[:, None, :], 'dp', split_axis=2, concat_axis=...  15.8 us
    all_to_all x3, local copies, waits for them, and re-layouts, on_device(): lax.all_to_all(hidden_local[:, None, :], 'dp', split_axis=2, concat_axis=...  8.22 us
    another operation x1, local copies, waits for them, and re-layouts, on_device(): hidden_local[:, None, :]  5.94 us
    dot_general x1, matrix products, on_device(): lax.dot_general(left, right, (((0,), (0,)), ((), ())), preferred_element_...  5.47 us
    dot_general x1, matrix products, on_device(): lax.dot_general(rows, down_weight, (((1,), (1,)), ((), ())), preferred_el...  5.43 us
  transfers between devices with their start and end apart: 4, of which 2 were waited for; matrix products, arithmetic and copies ran while one was open for 39% of the time, Pallas kernels for 0%

commit v1 on v0

--- a/solution.py
+++ b/solution.py
@@ -14,8 +14,11 @@
     tok_count = grad_all.shape[0]
     replica_count = grad_all.shape[1]
     local_tokens = hidden_local.shape[0]
-    hidden_units = lax.all_to_all(
-        hidden_local[:, None, :], "dp", split_axis=2, concat_axis=1, tiled=True
+    hidden_units = jnp.concatenate(
+        lax.all_to_all(
+            jnp.stack(jnp.split(hidden_local[:, None, :], lax.axis_size("dp"), axis=2)), "dp", 0, 0
+        ),
+        axis=1,
     )
     factor = jnp.float32(1.0) / jnp.sqrt(jnp.float32(tok_count * replica_count))
     flat_grad = grad_all.reshape(tok_count * replica_count, width)

time: 170 us -> 132 us (0.78)
  other arithmetic: 39.8 us -> 0.06 us
  waiting for transfers between devices: 57.7 us -> 74.5 us
  local copies, waits for them, and re-layouts: 25.9 us -> 11.2 us
    unnamed x1 -> x0, other arithmetic: 39.8 us -> none
    reduce_scatter x1, waiting for transfers between devices: 0.02 us -> 15.4 us  [on_device(): lax.psum_scatter(lax.dot_general(rows, down_weight, (((1,), (1,)), ((), (...]
    all_to_all x3 -> x0, local copies, waits for them, and re-layouts: 8.22 us -> none  [on_device(): lax.all_to_all(hidden_local[:, None, :], 'dp', split_axis=2, concat_axis=...]
    another operation x1, local copies, waits for them, and re-layouts: 5.94 us -> 0.03 us  [on_device(): jnp.stack(jnp.split(hidden_local[:, None, :], lax.axis_size('dp'), axis=2))]
    unnamed x7 -> x4, local copies, waits for them, and re-layouts: 5.28 us -> 0.01 us
    all_gather x0 -> x1, local copies, waits for them, and re-layouts: none -> 3.6 us  [on_device(): lax.all_gather(hidden_units, 'row', axis=0, tiled=True).reshape(-1, units)]
  transfers between devices with their start and end apart: 4 -> 4, of which waited for: 2 -> 3; matrix products, arithmetic and copies ran while one was open for 39% -> 8% of each run, Pallas kernels for 0% -> 0%
where the time goes in v1:
time: 132 us
  waiting for transfers between devices  74.5 us (56%)
  blocking collectives  18.1 us (14%)
  between operations  13.8 us (10%)
  local copies, waits for them, and re-layouts  11.2 us (8%)
  matrix products  9.37 us (7%)
  starting transfers between devices  4.72 us (4%)
    all_gather x1, waiting for transfers between devices, on_device(): lax.all_gather(grad_replica[:, None, :], 'dp', axis=1, tiled=True)  30.7 us
    all_gather x1, waiting for transfers between devices, on_device(): lax.all_gather(hidden_units, 'row', axis=0, tiled=True).reshape(-1, units)  28.3 us
    all_to_all x1, blocking collectives, on_device(): lax.all_to_all(jnp.stack(jnp.split(hidden_local[:, None, :], lax.axis_siz...  15.8 us
    reduce_scatter x1, waiting for transfers between devices, on_device(): lax.psum_scatter(lax.dot_general(rows, down_weight, (((1,), (1,)), ((), (...  15.4 us
    dot_general x1, matrix products, on_device(): lax.dot_general(rows, down_weight, (((1,), (1,)), ((), ())), preferred_el...  5.43 us
    all_to_all x1, starting transfers between devices, on_device(): lax.all_to_all(local_grad, 'dp', split_axis=1, concat_axis=2, tiled=True)  4.6 us
    dot_general x1, matrix products, on_device(): lax.dot_general(left, right, (((0,), (0,)), ((), ())), preferred_element_...  3.94 us
    all_gather x1, local copies, waits for them, and re-layouts, on_device(): lax.all_gather(hidden_units, 'row', axis=0, tiled=True).reshape(-1, units)  3.6 us
  transfers between devices with their start and end apart: 4, of which 3 were waited for; matrix products, arithmetic and copies ran while one was open for 8% of the time, Pallas kernels for 0%

profile of v1, /device:TPU:0, one launch (start us, length us, event | category | flops | bytes accessed | tf_op | source)
XLA Modules:
  0.0 131.8 jit_solution(17426707782934796457)
XLA Ops:
  7.2 0.0 all-gather.6.cloned.1.call-start
  7.2 2.3 %all-gather = bf16[1,128,1024]{2,1,0:T(8,128)(2,1)S(1)} all-gather(bf16[1,64,1024]{2,1,0:T(8,128)(2,1)} %param.3), channel_id=2, replica_groups=mesh['row'=4,'col'=2,'dp'=4] {'col'}, dimensions={1}, use_global_device_ids=true | all-gather | bytes 393216 | tf_op jit(solution)/shard_map/all_gather | solution.py:12
  9.5 0.8 copy.28
  10.4 0.0 all-gather.6.cloned.1.call-update
  10.4 0.0 reduce-scatter.2.cloned.1.call-start
  10.5 30.7 %all-gather.6.cloned.1.call-done = bf16[1,128,4096]{1,2,0:T(8,128)(2,1)} async-done(((bf16[1,128,1024]{1,2,0:T(8,128)(2,1)}), bf16[1,128,4096]{1,2,0:T(8,128)(2,1)}) %all-gather.6.cloned.1.call-update) | async-done | bytes 1048592 | tf_op jit(solution)/shard_map/all_gather | solution.py:13
  41.1 1.5 %copy.29 = bf16[1,128,4096]{2,1,0:T(8,128)(2,1)S(1)} copy(bf16[1,128,4096]{1,2,0:T(8,128)(2,1)} %all-gather.6.cloned.1.call-done) | data formatting | bytes 2097152 | tf_op jit(solution)/shard_map/all_gather | solution.py:13
  42.6 0.7 reshape.25
  43.3 0.0 copy-start.1
  43.3 5.4 %convolution_convert_fusion = bf16[512,1792]{1,0:T(8,128)(2,1)} fusion(bf16[512,1024]{1,0:T(8,128)(2,1)S(1)} %reshape.25, bf16[1792,1024]{1,0:T(8,128)(2,1)} %param.5), kind=kOutput, calls=%fused_computation.2 | convolution fusion | flops 1879965696 | bytes 6553600 | tf_op jit(solution)/shard_map/dot_general | solution.py:27
  48.8 0.0 reduce-scatter.2.cloned.1.call-update
  48.8 0.0 all-gather.8.cloned.1.call-start
  48.8 0.0 copy-done.1
  48.9 0.1 pad_maximum_fusion
  49.0 15.8 %all_to_all.14 = bf16[4,32,1,1792]{3,1,2,0:T(8,128)(2,1)S(1)} all-to-all(bf16[4,32,1,1792]{3,1,2,0:T(8,128)(2,1)S(1)} %pad_maximum_fusion), channel_id=1, replica_groups=mesh['row'=4,'col'=2,'dp'=4] {'dp'}, dimensions={0} | all-to-all | bytes 917504 | tf_op jit(solution)/shard_map/all_to_all | solution.py:18
  64.8 1.1 copy.32
  65.9 0.0 copy-start
  65.9 0.0 all-gather.8.cloned.1.call-update
  65.9 15.4 %reduce-scatter.2.cloned.1.call-done = bf16[128,1792]{1,0:T(8,128)(2,1)} async-done(((bf16[512,1792]{1,0:T(8,128)(2,1)}), bf16[128,1792]{1,0:T(8,128)(2,1)}) %reduce-scatter.2.cloned.1.call-update) | async-done | bytes 458768 | tf_op jit(solution)/shard_map/reduce_scatter | solution.py:26
  81.3 1.1 reshape.26
  82.5 0.8 copy.30
  83.3 4.6 %all-to-all-start = ((bf16[32,4,1792]{2,0,1:T(8,128)(2,1)}), bf16[32,4,1792]{2,0,1:T(8,128)(2,1)S(1)}, u32[]{:S(2)}, u32[]{:S(2)}) async-start(bf16[32,4,1792]{2,0,1:T(8,128)(2,1)} %copy.30), calls=%async_computation.1 | async-start | bytes 917504 | tf_op jit(solution)/shard_map/all_to_all | solution.py:35
  87.9 28.3 %all-gather.8.cloned.1.call-done = bf16[128,4,1,1792]{3,1,2,0:T(4,128)(2,1)} async-done(((bf16[32,4,1,1792]{3,1,2,0:T(4,128)(2,1)}), bf16[128,4,1,1792]{3,1,2,0:T(4,128)(2,1)}) %all-gather.8.cloned.1.call-update) | async-done | bytes 1835024 | tf_op jit(solution)/shard_map/all_gather | solution.py:38
  116.2 3.6 %copy.33 = bf16[128,4,1,1792]{0,3,1,2:T(8,128)(2,1)S(1)} copy(bf16[128,4,1,1792]{3,1,2,0:T(4,128)(2,1)} %all-gather.8.cloned.1.call-done) | data formatting | bytes 3670016 | tf_op jit(solution)/shard_map/all_gather | solution.py:38
  119.8 0.0 copy-done
  119.8 3.9 %fusion = bf16[1792,1024]{1,0:T(8,128)(2,1)} fusion(bf16[128,4,1024]{0,2,1:T(8,128)(2,1)S(1)} %bitcast.22, bf16[128,4,1,1792]{0,3,1,2:T(8,128)(2,1)S(1)} %copy.33), kind=kOutput, calls=%fused_computation.1 | convolution fusion | flops 1882718208 | bytes 6553600 | tf_op jit(solution)/shard_map/dot_general | solution.py:40
  123.8 0.0 all-to-all-done
  123.8 0.4 copy.31
  124.2 1.1 reshape.27
  (1 shorter events, 0.0 us)
Async XLA Ops:
  7.2 34.0 %all-gather.6.cloned.1.call-start = ((), (), s32[]{:S(2)}) async-start(), calls=%async_computation.4 | async-start | bytes 1310720 | tf_op jit(solution)/shard_map/all_gather | solution.py:13
  10.4 70.9 %reduce-scatter.2.cloned.1.call-start = ((), (), s32[]{:S(2)}) async-start(), calls=%async_computation.3 | async-start | bytes 2293760 | tf_op jit(solution)/shard_map/reduce_scatter | solution.py:26
  43.3 5.5 %copy-start.1 = (bf16[1,32,7168]{2,1,0:T(8,128)(2,1)S(1)}, bf16[1,32,7168]{2,1,0:T(8,128)(2,1)}, u32[]{:S(2)}) copy-start(bf16[1,32,7168]{2,1,0:T(8,128)(2,1)} %param.4) | copy-start | bytes 1376260
  48.8 67.4 %all-gather.8.cloned.1.call-start = ((), (), s32[]{:S(2)}) async-start(), calls=%async_computation.5 | async-start | bytes 2293760 | tf_op jit(solution)/shard_map/all_gather | solution.py:38
  65.9 53.9 %copy-start = (bf16[1,128,4096]{1,2,0:T(8,128)(2,1)S(1)}, bf16[1,128,4096]{1,2,0:T(8,128)(2,1)}, u32[]{:S(2)}) copy-start(bf16[1,128,4096]{1,2,0:T(8,128)(2,1)} %all-gather.6.cloned.1.call-done) | copy-start | bytes 3145732
  83.3 40.5 %all-to-all-start = ((bf16[32,4,1792]{2,0,1:T(8,128)(2,1)}), bf16[32,4,1792]{2,0,1:T(8,128)(2,1)S(1)}, u32[]{:S(2)}, u32[]{:S(2)}) async-start(bf16[32,4,1792]{2,0,1:T(8,128)(2,1)} %copy.30), calls=%async_computation.1 | async-start | bytes 917504 | tf_op jit(solution)/shard_map/all_to_all | solution.py:35
Sparse Core Ops, SparseCore 0:
  10.5 30.5 all-gather.5
  48.9 32.3 reduce-scatter.1
  83.2 32.9 all-gather.7
